TPU v7x, 512 devices: a whole 4x4x16 slice. The times are simulated.
512 devices in a mesh: img: 32 (over x, z_hi, core), py: 4 (over y), px: 4 (over z_lo).
Axes of the slice: x: 4, y: 4, z: 16 (z_hi: 4, z_lo: 4; z = z_hi * 4 + z_lo), core: 2. Of those that a mesh axis runs over, the one named last changes fastest.
Arguments:
- queries: bfloat16 [32, 64, 64, 1536], P('img', 'py', 'px')
- keys: bfloat16 [32, 64, 64, 1536], P('img', 'py', 'px')
- values: bfloat16 [32, 64, 64, 1536], P('img', 'py', 'px'), may hold values from -6 to 6
- pattern: int32 [32, 8, 8, 9], P('img', 'py', 'px'), may hold values from 0 to 1, as said below
- targets: int32 [32, 8, 8, 12, 3], P('img', 'py', 'px'), may hold values from 0 to 8, as said below
- router_q: float32 [12, 128, 64], replicated, may hold values from -1.5 to 1.5
- router_k: float32 [12, 128, 64], replicated, may hold values from -1.5 to 1.5
Outputs:
- attended: bfloat16 [32, 64, 64, 1536], P('img', 'py', 'px')
- grad_q: float32 [12, 128, 64], replicated
- grad_k: float32 [12, 128, 64], replicated
Inputs may be any that keep to these rules, and one draw needn't show every extreme that they name: `pattern`: the centre offset and the offsets one block away along one axis that lie in the image are 1; offsets outside the image are 0. `targets`: 3 different offsets per query block and head, each with pattern 1.
All inputs are finite; a program needn't handle non-finite values.
Results may differ from a plain program's by a relative error of at most 0.0049.
Values may be sent and summed in bfloat16 or wider, within the bound.
No kernel may reach another device: no remote copies, remote signals or barrier semaphores. Data moves between devices by JAX's collectives and lax.ppermute only.
A program may use at most 64 MiB of HBM per device.

v0:
```python
import math
import jax
import jax.numpy as jnp
from jax import lax
from jax.sharding import PartitionSpec as P

HEADS = 12
DH = 128
RW = 64
BS = 8
RADIUS = 1
TOPK = 3
NOFF = 9


def extended_2(cells, sides, width):
    for axis, dim in sides:
        count = lax.axis_size(axis)
        ends = count - 1
        head = lax.slice_in_dim(cells, 0, width, axis=dim)
        tail = lax.slice_in_dim(cells, cells.shape[dim] - width, cells.shape[dim], axis=dim)
        cells = jnp.concatenate(
            [
                lax.ppermute(tail, axis, [(i, (i + 1) % count) for i in range(ends)]),
                cells,
                lax.ppermute(head, axis, [((i + 1) % count, i) for i in range(ends)]),
            ],
            axis=dim,
        )
    return cells


def attend(query_tile, key_ext, value_ext, live):
    tile_y, tile_x, feat = query_tile.shape
    blocks_y = tile_y // BS
    blocks_x = tile_x // BS
    width = 2 * RADIUS + 1
    side = width * BS
    scale = 1.0 / math.sqrt(DH)
    anchor = jnp.zeros((), jnp.int32)

    def regroup(window):
        return (
            window.reshape(width, BS, width, BS, feat)
            .transpose(0, 2, 1, 3, 4)
            .reshape(NOFF * BS * BS, HEADS, DH)
        )

    def one_block(index):
        row = index // blocks_x
        col = index % blocks_x
        start_y = row * BS
        start_x = col * BS
        query = lax.dynamic_slice(query_tile, (start_y, start_x, anchor), (BS, BS, feat)).reshape(
            BS * BS, HEADS, DH
        )
        window_k = regroup(
            lax.dynamic_slice(key_ext, (start_y, start_x, anchor), (side, side, feat))
        )
        window_v = regroup(
            lax.dynamic_slice(value_ext, (start_y, start_x, anchor), (side, side, feat))
        )
        mask_row = lax.dynamic_slice(live, (row, col, anchor), (1, 1, NOFF)).reshape(NOFF)
        key_mask = jnp.repeat(mask_row, BS * BS) > 0
        scores = (
            jnp.einsum("qhd,khd->hqk", query, window_k, preferred_element_type=jnp.float32) * scale
        )
        scores = jnp.where(key_mask[None, None, :], scores, -1e30)
        top = jnp.max(scores, axis=-1, keepdims=True)
        weights = jnp.exp(scores - top)
        probs = (weights / jnp.sum(weights, axis=-1, keepdims=True)).astype(jnp.bfloat16)
        out = jnp.einsum("hqk,khd->qhd", probs, window_v, preferred_element_type=jnp.float32)
        return out.astype(jnp.bfloat16).reshape(BS, BS, feat)

    outs = lax.map(one_block, jnp.arange(blocks_y * blocks_x, dtype=jnp.int32))
    return (
        outs.reshape(blocks_y, blocks_x, BS, BS, feat)
        .transpose(0, 2, 1, 3, 4)
        .reshape(tile_y, tile_x, feat)
    )


def pooling(tile):
    tile_y, tile_x, feat = tile.shape
    shaped = tile.reshape(tile_y // BS, BS, tile_x // BS, BS, HEADS, DH)
    return jnp.sum(shaped, axis=(1, 3), dtype=jnp.float32) / (BS * BS)


def router_loss(weights_q, weights_k, pooled_q, pooled_k, live, chosen):
    route_q = jnp.einsum("yxhd,hdr->yxhr", pooled_q, weights_q, precision=lax.Precision.HIGHEST)
    route_k = jnp.einsum("yxhd,hdr->yxhr", pooled_k, weights_k, precision=lax.Precision.HIGHEST)
    blocks_y, blocks_x = (pooled_q.shape[0], pooled_q.shape[1])
    width = 2 * RADIUS + 1
    shifted = jnp.stack(
        [
            route_k[up : up + blocks_y, left : left + blocks_x]
            for up in range(width)
            for left in range(width)
        ],
        axis=2,
    )
    logits = jnp.einsum(
        "yxhr,yxohr->yxho", route_q, shifted, precision=lax.Precision.HIGHEST
    ) / math.sqrt(RW)
    logits = jnp.where(live[:, :, None, :] > 0, logits, -1e30)
    top = jnp.max(logits, axis=-1, keepdims=True)
    logz = top + jnp.log(jnp.sum(jnp.exp(logits - top), axis=-1, keepdims=True))
    logp = logits - logz
    picks = (chosen[..., None] == jnp.arange(NOFF, dtype=jnp.int32)).astype(jnp.float32)
    return -jnp.sum(picks * logp[:, :, :, None, :])


def per_device(queries, keys, values, pattern, targets, router_q, router_k):
    rim = RADIUS * BS
    stacked = jnp.stack([keys, values])
    extended = extended_2(stacked, (("py", 2), ("px", 3)), rim)
    key_ext = extended[0, 0]
    value_ext = extended[1, 0]
    attended = attend(queries[0], key_ext, value_ext, pattern[0])[None]
    pooled_q = pooling(queries[0])
    pooled_k = pooling(key_ext)
    blocks_y = pooled_q.shape[0]
    blocks_x = pooled_q.shape[1]
    normal = float(TOPK * HEADS * blocks_y * lax.axis_size("py") * blocks_x * lax.axis_size("px"))

    def local_loss(weights_q, weights_k):
        return (
            router_loss(weights_q, weights_k, pooled_q, pooled_k, pattern[0], targets[0]) / normal
        )

    grad_q, grad_k = jax.grad(local_loss, argnums=(0, 1))(router_q, router_k)
    grad_q, grad_k = lax.psum((grad_q, grad_k), ("img", "py", "px"))
    return (attended, grad_q, grad_k)


def solution(mesh):
    return jax.shard_map(
        per_device,
        mesh=mesh,
        in_specs=(
            P("img", "py", "px", None),
            P("img", "py", "px", None),
            P("img", "py", "px", None),
            P("img", "py", "px", None),
            P("img", "py", "px", None, None),
            P(),
            P(),
        ),
        out_specs=(P("img", "py", "px", None), P(), P()),
        check_vma=False,
    )
```

profile of v0, /device:TPU:2, one launch (start us, length us, event | category | flops | bytes accessed | tf_op | source)
XLA Modules:
  0.0 595.2 jit_solution(9057163803612186937)
XLA Ops:
  8.9 3.5 collective-permute-start
  13.7 15.4 %collective-permute-done = bf16[2,1,8,16,1536]{4,3,2,1,0:T(8,128)(2,1)S(1)} collective-permute-done((bf16[2,1,8,16,1536]{4,3,2,1,0:T(8,128)(2,1)S(1)}, bf16[2,1,8,16,1536]{4,3,2,1,0:T(8,128)(2,1)S(1)}, u32[]{:S(2)}, u32[]{:S(2)}) %collective-permute-start) | collective-permute-done | bytes 786464 | tf_op jit(solution)/shard_map/ppermute | solution.py:24
  29.1 4.2 collective-permute-done.1
  34.6 1.9 fusion.85
  36.5 5.0 collective-permute-start.2
  46.2 26.9 %collective-permute-done.2 = bf16[2,1,32,8,1536]{4,3,2,1,0:T(8,128)(2,1)} collective-permute-done((bf16[2,1,32,8,1536]{4,3,2,1,0:T(8,128)(2,1)}, bf16[2,1,32,8,1536]{4,3,2,1,0:T(8,128)(2,1)}, u32[]{:S(2)}, u32[]{:S(2)}) %collective-permute-start.2) | collective-permute-done | bytes 1572896 | tf_op jit(solution)/shard_map/ppermute | solution.py:24
  73.2 5.3 collective-permute-done.3
  78.5 3.2 pad_maximum_fusion
  81.6 2.4 fusion.84
  100.1 2.3 convolution_bitcast_fusion
  102.5 2.6 convolution_bitcast_fusion.1
  105.1 122.5 %while.12 = (s32[]{:T(128)}, bf16[4,8,8,1536]{3,2,1,0:T(8,128)(2,1)}, s32[4]{0:T(128)S(1)}, bf16[32,32,1536]{2,1,0:T(8,128)(2,1)}, s32[2,2,9]{2,1,0:T(2,128)S(1)...) while((s32[]{:T(128)}, ...), condition=%wide.region_3.4_spmd, body=%wide.region_0.3_spmd.sunk | while | flops 343820224 | bytes 57812960 | solution.py:75
  108.5 3.0 constant_dynamic-slice_fusion.6
  113.0 3.0 reshape.102
  117.1 2.2 fusion.101
  119.5 2.0 fusion.100
  123.2 2.7 reshape.101
  125.9 4.7 fusion.102
  130.6 1.8 copy.119
  132.3 1.8 broadcast_in_dim.131
  139.1 3.1 constant_dynamic-slice_fusion.6
  143.6 3.0 reshape.102
  147.7 2.2 fusion.101
  150.2 2.0 fusion.100
  153.8 2.7 reshape.101
  156.5 4.7 fusion.102
  161.2 1.8 copy.119
  163.0 1.8 broadcast_in_dim.131
  169.7 3.0 constant_dynamic-slice_fusion.6
  174.2 3.0 reshape.102
  178.4 2.2 fusion.101
  180.8 2.0 fusion.100
  184.4 2.7 reshape.101
  187.1 4.7 fusion.102
  191.8 1.8 copy.119
  193.6 1.8 broadcast_in_dim.131
  200.3 3.1 constant_dynamic-slice_fusion.6
  204.9 3.0 reshape.102
  209.0 2.2 fusion.101
  211.4 2.0 fusion.100
  215.1 2.7 reshape.101
  217.8 4.7 fusion.102
  222.5 1.8 copy.119
  224.2 1.8 broadcast_in_dim.131
  227.6 2.1 copy.48
  229.7 355.1 %all-reduce.12.cloned.1.call-done = (f32[12,128,64]{1,2,0:T(8,128)}, f32[12,128,64]{1,2,0:T(8,128)}) async-done(((f32[12,128,64]{1,2,0:T(8,128)}, f32[12,128,64]{1,2,0:T(8,128)}), (f32[12,128,64]{1,2,0:T(8,128)}, f32[12,128,64]{1,2,0:T(8,128)})) %all-reduce.12.cloned.1.call-update) | async-done | bytes 786448 | tf_op jit(solution)/shard_map/psum | solution.py:132
  584.8 1.8 copy.137
  586.6 1.8 copy.138
  (111 shorter events, 51.6 us)
Async XLA Ops:
  7.2 78.1 %copy-start = (f32[12,128,64]{1,2,0:T(8,128)S(1)}, f32[12,128,64]{1,2,0:T(8,128)}, u32[]{:S(2)}) copy-start(f32[12,128,64]{1,2,0:T(8,128)} %param.15) | copy-start | bytes 1179652
  7.2 27.0 %copy-start.3 = (bf16[1,16,16,1536]{3,2,1,0:T(8,128)(2,1)S(1)}, bf16[1,16,16,1536]{3,2,1,0:T(8,128)(2,1)}, u32[]{:S(2)}) copy-start(bf16[1,16,16,1536]{3,2,1,0:T(8,128)(2,1)} %param.10) | copy-start | bytes 2359300
  7.2 27.0 %copy-start.4 = (bf16[1,16,16,1536]{3,2,1,0:T(8,128)(2,1)S(1)}, bf16[1,16,16,1536]{3,2,1,0:T(8,128)(2,1)}, u32[]{:S(2)}) copy-start(bf16[1,16,16,1536]{3,2,1,0:T(8,128)(2,1)} %param.11) | copy-start | bytes 2359300
  7.2 577.6 %all-reduce.12.cloned.1.call-start = ((), (), s32[]{:S(2)}) async-start(), calls=%async_computation | async-start | bytes 1572864 | tf_op jit(solution)/shard_map/psum | solution.py:132
  8.9 20.3 %collective-permute-start = (bf16[2,1,8,16,1536]{4,3,2,1,0:T(8,128)(2,1)S(1)}, bf16[2,1,8,16,1536]{4,3,2,1,0:T(8,128)(2,1)S(1)}, u32[]{:S(2)}, u32[]{:S(2)}) collective-permute-start(bf16[2,1,8,16,1536]{4,3,2,1,0:T(8,128)(2,1)S(1)} %get-tuple-element.123), channel_id=1, source_target_pairs={{0,4},{4,8},{8,12},{1,5},{5,9},{9,13},{2,6},{6,10},{10,14},{3,7},{... | collective-permute-start | bytes 2359304 | tf_op jit(solution)/shard_map/ppermute | solution.py:24
  12.4 20.9 %collective-permute-start.1 = (bf16[2,1,8,16,1536]{4,3,2,1,0:T(8,128)(2,1)S(1)}, bf16[2,1,8,16,1536]{4,3,2,1,0:T(8,128)(2,1)S(1)}, u32[]{:S(2)}, u32[]{:S(2)}) collective-permute-start(bf16[2,1,8,16,1536]{4,3,2,1,0:T(8,128)(2,1)S(1)} %get-tuple-element.124), channel_id=1, source_target_pairs={{4,0},{8,4},{12,8},{5,1},{9,5},{13,9},{6,2},{10,6},{14,10},{7,3},{... | collective-permute-start | bytes 2359304 | tf_op jit(solution)/shard_map/ppermute | solution.py:26
  33.3 0.9 copy-start.6
  34.6 8.2 %copy-start.11 = (s32[1,2,2,9]{3,2,1,0:T(2,128)S(1)}, s32[1,2,2,9]{3,2,1,0:T(2,128)}, u32[]{:S(2)}) copy-start(s32[1,2,2,9]{3,2,1,0:T(2,128)} %param.12) | copy-start | bytes 436
  34.6 9.7 %copy-start.5 = (bf16[1,16,16,1536]{3,2,1,0:T(8,128)(2,1)S(1)}, bf16[1,16,16,1536]{3,2,1,0:T(8,128)(2,1)}, u32[]{:S(2)}) copy-start(bf16[1,16,16,1536]{3,2,1,0:T(8,128)(2,1)} %param.9) | copy-start | bytes 2359300
  36.5 36.6 %collective-permute-start.2 = (bf16[2,1,32,8,1536]{4,3,2,1,0:T(8,128)(2,1)}, bf16[2,1,32,8,1536]{4,3,2,1,0:T(8,128)(2,1)}, u32[]{:S(2)}, u32[]{:S(2)}) collective-permute-start(bf16[2,1,32,8,1536]{4,3,2,1,0:T(8,128)(2,1)} %get-tuple-element.121), channel_id=1, source_target_pairs={{0,1},{1,2},{2,3},{4,5},{5,6},{6,7},{8,9},{9,10},{10,11},{12,13},{... | collective-permute-start | bytes 4718600 | tf_op jit(solution)/shard_map/ppermute | solution.py:24
  41.5 36.9 %collective-permute-start.3 = (bf16[2,1,32,8,1536]{4,3,2,1,0:T(8,128)(2,1)}, bf16[2,1,32,8,1536]{4,3,2,1,0:T(8,128)(2,1)}, u32[]{:S(2)}, u32[]{:S(2)}) collective-permute-start(bf16[2,1,32,8,1536]{4,3,2,1,0:T(8,128)(2,1)} %get-tuple-element.122), channel_id=1, source_target_pairs={{1,0},{2,1},{3,2},{5,4},{6,5},{7,6},{9,8},{10,9},{11,10},{13,12},{... | collective-permute-start | bytes 4718600 | tf_op jit(solution)/shard_map/ppermute | solution.py:26
  44.5 34.0 %copy-start.10 = (f32[2,2,12,128]{3,2,1,0:T(8,128)}, f32[2,2,12,128]{3,2,1,0:T(8,128)S(1)}, u32[]{:S(2)}) copy-start(f32[2,2,12,128]{3,2,1,0:T(8,128)S(1)} %broadcast_multiply_fusion.1) | copy-start | bytes 73732
  46.2 40.1 %copy-start.9 = (f32[12,2,2,64]{3,2,1,0:T(2,128)}, f32[12,2,2,64]{3,2,1,0:T(2,128)S(1)}, u32[]{:S(2)}) copy-start(f32[12,2,2,64]{3,2,1,0:T(2,128)S(1)} %fusion.37) | copy-start | bytes 36868
  84.6 0.7 copy-start.8
  86.3 0.7 copy-start.7
  105.1 6.4 %copy-start.1 = (bf16[32,32,1536]{2,1,0:T(8,128)(2,1)}, bf16[32,32,1536]{2,1,0:T(8,128)(2,1)S(1)}, u32[]{:S(2)}) copy-start(bf16[32,32,1536]{2,1,0:T(8,128)(2,1)S(1)} %get-tuple-element.215) | copy-start | bytes 9437188 | tf_op jit(solution)/shard_map/while
  125.9 9.8 %copy-start.2 = (bf16[32,32,1536]{2,1,0:T(8,128)(2,1)S(1)}, bf16[32,32,1536]{2,1,0:T(8,128)(2,1)}, u32[]{:S(2)}) copy-start(bf16[32,32,1536]{2,1,0:T(8,128)(2,1)} %copy-done.1) | copy-start | bytes 9437188 | tf_op jit(solution)/shard_map/while
  135.7 6.4 %copy-start.1 = (bf16[32,32,1536]{2,1,0:T(8,128)(2,1)}, bf16[32,32,1536]{2,1,0:T(8,128)(2,1)S(1)}, u32[]{:S(2)}) copy-start(bf16[32,32,1536]{2,1,0:T(8,128)(2,1)S(1)} %get-tuple-element.215) | copy-start | bytes 9437188 | tf_op jit(solution)/shard_map/while
  156.5 9.9 %copy-start.2 = (bf16[32,32,1536]{2,1,0:T(8,128)(2,1)S(1)}, bf16[32,32,1536]{2,1,0:T(8,128)(2,1)}, u32[]{:S(2)}) copy-start(bf16[32,32,1536]{2,1,0:T(8,128)(2,1)} %copy-done.1) | copy-start | bytes 9437188 | tf_op jit(solution)/shard_map/while
  166.4 6.4 %copy-start.1 = (bf16[32,32,1536]{2,1,0:T(8,128)(2,1)}, bf16[32,32,1536]{2,1,0:T(8,128)(2,1)S(1)}, u32[]{:S(2)}) copy-start(bf16[32,32,1536]{2,1,0:T(8,128)(2,1)S(1)} %get-tuple-element.215) | copy-start | bytes 9437188 | tf_op jit(solution)/shard_map/while
  187.1 9.9 %copy-start.2 = (bf16[32,32,1536]{2,1,0:T(8,128)(2,1)S(1)}, bf16[32,32,1536]{2,1,0:T(8,128)(2,1)}, u32[]{:S(2)}) copy-start(bf16[32,32,1536]{2,1,0:T(8,128)(2,1)} %copy-done.1) | copy-start | bytes 9437188 | tf_op jit(solution)/shard_map/while
  197.0 6.4 %copy-start.1 = (bf16[32,32,1536]{2,1,0:T(8,128)(2,1)}, bf16[32,32,1536]{2,1,0:T(8,128)(2,1)S(1)}, u32[]{:S(2)}) copy-start(bf16[32,32,1536]{2,1,0:T(8,128)(2,1)S(1)} %get-tuple-element.215) | copy-start | bytes 9437188 | tf_op jit(solution)/shard_map/while
  217.8 9.8 %copy-start.2 = (bf16[32,32,1536]{2,1,0:T(8,128)(2,1)S(1)}, bf16[32,32,1536]{2,1,0:T(8,128)(2,1)}, u32[]{:S(2)}) copy-start(bf16[32,32,1536]{2,1,0:T(8,128)(2,1)} %copy-done.1) | copy-start | bytes 9437188 | tf_op jit(solution)/shard_map/while
Sparse Core Ops, SparseCore 0:
  105.2 479.5 all-reduce.11
where the time goes:
time: 597 us; the launch traced here: 595 us
  waiting for transfers between devices  407 us (68%)
  local copies, waits for them, and re-layouts  93.3 us (16%)
  matrix products  46.1 us (8%)
  between operations  14.3 us (2%)
  other arithmetic  12.5 us (2%)
  starting transfers between devices  11.1 us (2%)
  loops' own time  10.9 us (2%)
    psum x1, waiting for transfers between devices, per_device(): grad_q, grad_k = lax.psum((grad_q, grad_k), ('img', 'py', 'px'))  355 us
    ppermute x2, waiting for transfers between devices, extended_2(): lax.ppermute(tail, axis, [(i, (i + 1) % count) for i in range(ends)])  42.4 us
    reshape x8, local copies, waits for them, and re-layouts, regroup(): return window.reshape(width, BS, width, BS, feat).transpose(0, 2, 1, 3, 4...  22.8 us
    dot_general x4, matrix products, one_block(): jnp.einsum('hqk,khd->qhd', probs, window_v, preferred_element_type=jnp.fl...  18.8 us
    transpose x8, local copies, waits for them, and re-layouts, regroup(): return window.reshape(width, BS, width, BS, feat).transpose(0, 2, 1, 3, 4...  12.4 us
    dynamic_slice x4, local copies, waits for them, and re-layouts, one_block(): lax.dynamic_slice(key_ext, (start_y, start_x, anchor), (side, side, feat))  12.2 us
  transfers between devices with their start and end apart: 5, of which 5 were waited for; matrix products, arithmetic and copies ran while one was open for 20% of the time, Pallas kernels for 0%

commit v1 on v0

--- a/solution.py
+++ b/solution.py
@@ -1,3 +1,4 @@
+import functools
 import math
 import jax
 import jax.numpy as jnp
@@ -11,6 +12,15 @@
 RADIUS = 1
 TOPK = 3
 NOFF = 9
+
+
+def list_indices(field_in, axis_tag, along_axis):
+    for c in (axis_tag, along_axis):
+        field_in = jax.lax.psum(field_in, c)
+    return field_in
+
+
+time_skins = functools.partial(list_indices, axis_tag=("py", "px"), along_axis="img")
 
 
 def extended_2(cells, sides, width):
@@ -129,7 +139,7 @@
         )
 
     grad_q, grad_k = jax.grad(local_loss, argnums=(0, 1))(router_q, router_k)
-    grad_q, grad_k = lax.psum((grad_q, grad_k), ("img", "py", "px"))
+    grad_q, grad_k = time_skins((grad_q, grad_k))
     return (attended, grad_q, grad_k)
 
 

time: 597 us -> 646 us (1.082)
  the two profiles are of different devices: /device:TPU:2 before, /device:TPU:1 now
where the time goes in v1:
time: 646 us; the launch traced here: 644 us
  waiting for transfers between devices  452 us (70%)
  local copies, waits for them, and re-layouts  93.2 us (14%)
  matrix products  46.1 us (7%)
  starting transfers between devices  14.8 us (2%)
  between operations  14.3 us (2%)
  other arithmetic  12.5 us (2%)
  loops' own time  10.9 us (2%)
    psum x2, waiting for transfers between devices, list_indices(): field_in = jax.lax.psum(field_in, c)  405 us
    ppermute x2, waiting for transfers between devices, extended_2(): lax.ppermute(tail, axis, [(i, (i + 1) % count) for i in range(ends)])  38.1 us
    reshape x8, local copies, waits for them, and re-layouts, regroup(): return window.reshape(width, BS, width, BS, feat).transpose(0, 2, 1, 3, 4...  22.8 us
    dot_general x4, matrix products, one_block(): jnp.einsum('hqk,khd->qhd', probs, window_v, preferred_element_type=jnp.fl...  18.8 us
  transfers between devices with their start and end apart: 6, of which 6 were waited for; matrix products, arithmetic and copies ran while one was open for 18% of the time, Pallas kernels for 0%

profile of v1, /device:TPU:1, one launch (start us, length us, event | category | flops | bytes accessed | tf_op | source)
XLA Modules:
  0.0 644.2 jit_solution(15841915333563884405)
XLA Ops:
  8.9 4.1 collective-permute-start
  14.2 11.7 %collective-permute-done = bf16[2,1,8,16,1536]{4,3,2,1,0:T(8,128)(2,1)S(1)} collective-permute-done((bf16[2,1,8,16,1536]{4,3,2,1,0:T(8,128)(2,1)S(1)}, bf16[2,1,8,16,1536]{4,3,2,1,0:T(8,128)(2,1)S(1)}, u32[]{:S(2)}, u32[]{:S(2)}) %collective-permute-start) | collective-permute-done | bytes 786464 | tf_op jit(solution)/shard_map/ppermute | solution.py:34
  25.9 3.9 collective-permute-done.1
  31.2 1.9 fusion.85
  33.1 7.9 %collective-permute-start.2 = (bf16[2,1,32,8,1536]{4,3,2,1,0:T(8,128)(2,1)}, bf16[2,1,32,8,1536]{4,3,2,1,0:T(8,128)(2,1)}, u32[]{:S(2)}, u32[]{:S(2)}) collective-permute-start(bf16[2,1,32,8,1536]{4,3,2,1,0:T(8,128)(2,1)} %get-tuple-element.123), channel_id=1, source_target_pairs={{0,1},{1,2},{2,3},{4,5},{5,6},{6,7},{8,9},{9,10},{10,11},{12,13},{... | collective-permute-start | bytes 4718600 | tf_op jit(solution)/shard_map/ppermute | solution.py:34
  45.6 26.4 %collective-permute-done.2 = bf16[2,1,32,8,1536]{4,3,2,1,0:T(8,128)(2,1)} collective-permute-done((bf16[2,1,32,8,1536]{4,3,2,1,0:T(8,128)(2,1)}, bf16[2,1,32,8,1536]{4,3,2,1,0:T(8,128)(2,1)}, u32[]{:S(2)}, u32[]{:S(2)}) %collective-permute-start.2) | collective-permute-done | bytes 1572896 | tf_op jit(solution)/shard_map/ppermute | solution.py:34
  72.0 5.0 collective-permute-done.3
  77.0 3.2 pad_maximum_fusion
  80.2 2.4 fusion.84
  98.7 2.3 convolution_bitcast_fusion
  101.0 2.6 convolution_bitcast_fusion.1
  103.9 169.9 %all-reduce.16.cloned.1.call-done = (f32[12,128,64]{1,2,0:T(8,128)}, f32[12,128,64]{1,2,0:T(8,128)}) async-done(((f32[12,128,64]{1,2,0:T(8,128)}, f32[12,128,64]{1,2,0:T(8,128)}), (f32[12,128,64]{1,2,0:T(8,128)}, f32[12,128,64]{1,2,0:T(8,128)})) %all-reduce.16.cloned.1.call-update) | async-done | bytes 786448 | tf_op jit(solution)/shard_map/psum | solution.py:19
  273.8 122.4 %while.12 = (s32[]{:T(128)}, bf16[4,8,8,1536]{3,2,1,0:T(8,128)(2,1)}, s32[4]{0:T(128)S(1)}, bf16[32,32,1536]{2,1,0:T(8,128)(2,1)}, s32[2,2,9]{2,1,0:T(2,128)S(1)...) while((s32[]{:T(128)}, ...), condition=%wide.region_3.4_spmd, body=%wide.region_0.3_spmd.sunk | while | flops 343820224 | bytes 57812960 | solution.py:85
  277.2 3.0 constant_dynamic-slice_fusion.6
  281.7 3.0 reshape.102
  285.8 2.2 fusion.101
  288.3 2.0 fusion.100
  291.9 2.7 reshape.101
  294.6 4.7 fusion.102
  299.3 1.8 copy.119
  301.0 1.8 broadcast_in_dim.131
  307.8 3.0 constant_dynamic-slice_fusion.6
  312.3 3.0 reshape.102
  316.4 2.2 fusion.101
  318.9 2.0 fusion.100
  322.5 2.7 reshape.101
  325.2 4.7 fusion.102
  329.9 1.8 copy.119
  331.6 1.8 broadcast_in_dim.131
  338.4 3.0 constant_dynamic-slice_fusion.6
  342.9 3.0 reshape.102
  347.0 2.2 fusion.101
  349.4 2.0 fusion.100
  353.1 2.7 reshape.101
  355.8 4.7 fusion.102
  360.5 1.8 copy.119
  362.2 1.8 broadcast_in_dim.131
  369.0 3.1 constant_dynamic-slice_fusion.6
  373.5 3.0 reshape.102
  377.7 2.2 fusion.101
  380.1 2.0 fusion.100
  383.7 2.7 reshape.101
  386.4 4.7 fusion.102
  392.9 1.8 broadcast_in_dim.131
  396.3 2.1 copy.48
  398.3 235.5 %all-reduce.14.cloned.1.call-done = (f32[12,128,64]{1,2,0:T(8,128)}, f32[12,128,64]{1,2,0:T(8,128)}) async-done(((f32[12,128,64]{1,2,0:T(8,128)}, f32[12,128,64]{1,2,0:T(8,128)}), (f32[12,128,64]{1,2,0:T(8,128)}, f32[12,128,64]{1,2,0:T(8,128)})) %all-reduce.14.cloned.1.call-update) | async-done | bytes 786448 | tf_op jit(solution)/shard_map/psum | solution.py:19
  633.8 1.8 copy.139
  635.6 1.8 copy.140
  (114 shorter events, 53.6 us)
Async XLA Ops:
  7.2 76.7 %copy-start = (f32[12,128,64]{1,2,0:T(8,128)S(1)}, f32[12,128,64]{1,2,0:T(8,128)}, u32[]{:S(2)}) copy-start(f32[12,128,64]{1,2,0:T(8,128)} %param.15) | copy-start | bytes 1179652
  7.2 23.5 %copy-start.3 = (bf16[1,16,16,1536]{3,2,1,0:T(8,128)(2,1)S(1)}, bf16[1,16,16,1536]{3,2,1,0:T(8,128)(2,1)}, u32[]{:S(2)}) copy-start(bf16[1,16,16,1536]{3,2,1,0:T(8,128)(2,1)} %param.10) | copy-start | bytes 2359300
  7.2 23.5 %copy-start.4 = (bf16[1,16,16,1536]{3,2,1,0:T(8,128)(2,1)S(1)}, bf16[1,16,16,1536]{3,2,1,0:T(8,128)(2,1)}, u32[]{:S(2)}) copy-start(bf16[1,16,16,1536]{3,2,1,0:T(8,128)(2,1)} %param.11) | copy-start | bytes 2359300
  7.2 266.6 %all-reduce.16.cloned.1.call-start = ((), (), s32[]{:S(2)}) async-start(), calls=%async_computation.1 | async-start | bytes 1572864 | tf_op jit(solution)/shard_map/psum | solution.py:19
  8.9 17.1 %collective-permute-start = (bf16[2,1,8,16,1536]{4,3,2,1,0:T(8,128)(2,1)S(1)}, bf16[2,1,8,16,1536]{4,3,2,1,0:T(8,128)(2,1)S(1)}, u32[]{:S(2)}, u32[]{:S(2)}) collective-permute-start(bf16[2,1,8,16,1536]{4,3,2,1,0:T(8,128)(2,1)S(1)} %get-tuple-element.125), channel_id=1, source_target_pairs={{0,4},{4,8},{8,12},{1,5},{5,9},{9,13},{2,6},{6,10},{10,14},{3,7},{... | collective-permute-start | bytes 2359304 | tf_op jit(solution)/shard_map/ppermute | solution.py:34
  12.9 16.9 %collective-permute-start.1 = (bf16[2,1,8,16,1536]{4,3,2,1,0:T(8,128)(2,1)S(1)}, bf16[2,1,8,16,1536]{4,3,2,1,0:T(8,128)(2,1)S(1)}, u32[]{:S(2)}, u32[]{:S(2)}) collective-permute-start(bf16[2,1,8,16,1536]{4,3,2,1,0:T(8,128)(2,1)S(1)} %get-tuple-element.126), channel_id=1, source_target_pairs={{4,0},{8,4},{12,8},{5,1},{9,5},{13,9},{6,2},{10,6},{14,10},{7,3},{... | collective-permute-start | bytes 2359304 | tf_op jit(solution)/shard_map/ppermute | solution.py:36
  29.8 0.9 copy-start.6
  31.1 11.1 %copy-start.11 = (s32[1,2,2,9]{3,2,1,0:T(2,128)S(1)}, s32[1,2,2,9]{3,2,1,0:T(2,128)}, u32[]{:S(2)}) copy-start(s32[1,2,2,9]{3,2,1,0:T(2,128)} %param.12) | copy-start | bytes 436
  31.1 12.6 %copy-start.5 = (bf16[1,16,16,1536]{3,2,1,0:T(8,128)(2,1)S(1)}, bf16[1,16,16,1536]{3,2,1,0:T(8,128)(2,1)}, u32[]{:S(2)}) copy-start(bf16[1,16,16,1536]{3,2,1,0:T(8,128)(2,1)} %param.9) | copy-start | bytes 2359300
  33.1 38.9 %collective-permute-start.2 = (bf16[2,1,32,8,1536]{4,3,2,1,0:T(8,128)(2,1)}, bf16[2,1,32,8,1536]{4,3,2,1,0:T(8,128)(2,1)}, u32[]{:S(2)}, u32[]{:S(2)}) collective-permute-start(bf16[2,1,32,8,1536]{4,3,2,1,0:T(8,128)(2,1)} %get-tuple-element.123), channel_id=1, source_target_pairs={{0,1},{1,2},{2,3},{4,5},{5,6},{6,7},{8,9},{9,10},{10,11},{12,13},{... | collective-permute-start | bytes 4718600 | tf_op jit(solution)/shard_map/ppermute | solution.py:34
  40.9 36.1 %collective-permute-start.3 = (bf16[2,1,32,8,1536]{4,3,2,1,0:T(8,128)(2,1)}, bf16[2,1,32,8,1536]{4,3,2,1,0:T(8,128)(2,1)}, u32[]{:S(2)}, u32[]{:S(2)}) collective-permute-start(bf16[2,1,32,8,1536]{4,3,2,1,0:T(8,128)(2,1)} %get-tuple-element.124), channel_id=1, source_target_pairs={{1,0},{2,1},{3,2},{5,4},{6,5},{7,6},{9,8},{10,9},{11,10},{13,12},{... | collective-permute-start | bytes 4718600 | tf_op jit(solution)/shard_map/ppermute | solution.py:36
  43.9 33.1 %copy-start.10 = (f32[2,2,12,128]{3,2,1,0:T(8,128)}, f32[2,2,12,128]{3,2,1,0:T(8,128)S(1)}, u32[]{:S(2)}) copy-start(f32[2,2,12,128]{3,2,1,0:T(8,128)S(1)} %broadcast_multiply_fusion.1) | copy-start | bytes 73732
  45.6 39.2 %copy-start.9 = (f32[12,2,2,64]{3,2,1,0:T(2,128)}, f32[12,2,2,64]{3,2,1,0:T(2,128)S(1)}, u32[]{:S(2)}) copy-start(f32[12,2,2,64]{3,2,1,0:T(2,128)S(1)} %fusion.37) | copy-start | bytes 36868
  83.2 0.7 copy-start.8
  84.9 0.7 copy-start.7
  103.7 530.2 %all-reduce.14.cloned.1.call-start = ((), (), s32[]{:S(2)}) async-start(), calls=%async_computation | async-start | bytes 1572864 | tf_op jit(solution)/shard_map/psum | solution.py:19
  273.9 6.4 copy-start.1
  294.6 9.9 %copy-start.2 = (bf16[32,32,1536]{2,1,0:T(8,128)(2,1)S(1)}, bf16[32,32,1536]{2,1,0:T(8,128)(2,1)}, u32[]{:S(2)}) copy-start(bf16[32,32,1536]{2,1,0:T(8,128)(2,1)} %copy-done.1) | copy-start | bytes 9437188 | tf_op jit(solution)/shard_map/while
  304.4 6.4 copy-start.1
  325.2 9.9 %copy-start.2 = (bf16[32,32,1536]{2,1,0:T(8,128)(2,1)S(1)}, bf16[32,32,1536]{2,1,0:T(8,128)(2,1)}, u32[]{:S(2)}) copy-start(bf16[32,32,1536]{2,1,0:T(8,128)(2,1)} %copy-done.1) | copy-start | bytes 9437188 | tf_op jit(solution)/shard_map/while
  335.0 6.4 copy-start.1
  355.8 9.9 %copy-start.2 = (bf16[32,32,1536]{2,1,0:T(8,128)(2,1)S(1)}, bf16[32,32,1536]{2,1,0:T(8,128)(2,1)}, u32[]{:S(2)}) copy-start(bf16[32,32,1536]{2,1,0:T(8,128)(2,1)} %copy-done.1) | copy-start | bytes 9437188 | tf_op jit(solution)/shard_map/while
  365.6 6.4 copy-start.1
  386.4 9.8 %copy-start.2 = (bf16[32,32,1536]{2,1,0:T(8,128)(2,1)S(1)}, bf16[32,32,1536]{2,1,0:T(8,128)(2,1)}, u32[]{:S(2)}) copy-start(bf16[32,32,1536]{2,1,0:T(8,128)(2,1)} %copy-done.1) | copy-start | bytes 9437188 | tf_op jit(solution)/shard_map/while
Sparse Core Ops, SparseCore 0:
  103.8 169.9 all-reduce.15
  276.7 357.0 all-reduce.13
